TPU v7x, 512 devices: a whole 4x8x8 slice. The times are simulated.
512 devices in a mesh: tm: 128 (over y, x, z_lo, core), head: 4 (over z_hi).
Axes of the slice: x: 4, y: 8, z: 8 (z_hi: 4, z_lo: 2; z = z_hi * 2 + z_lo), core: 2. Of those that a mesh axis runs over, the one named last changes fastest.
Arguments:
- queries: bfloat16 [128, 128, 2048], P('tm', None, 'head'), may hold values from -6 to 6
- keys: bfloat16 [128, 128, 2048], P('tm', None, 'head'), may hold values from -6 to 6
- values: bfloat16 [128, 128, 2048], P('tm', None, 'head'), may hold values from -6 to 6
- anchor_of: int32 [128], replicated, may hold values from 0 to 126, as said below
- out_weight: bfloat16 [2048, 2048], P('head'), may hold values from -0.5 to 0.5
Outputs:
- mixed: bfloat16 [128, 128, 2048], P('tm', 'head')
Inputs may be any that keep to these rules, and one draw needn't show every extreme that they name: anchor_of[f] is the first frame of the segment that holds frame f; segments are runs of 1 to 4 frames, one of exactly 4; frame 0 starts a segment and the last segment has exactly 2 frames.
All inputs are finite; a program needn't handle non-finite values.
Results may differ from a plain program's by a relative error of at most 0.013.
Values may be sent and summed in bfloat16 or wider, within the bound.
A program may use at most 128 MiB of HBM per device.

v0:
```python
import jax
import jax.numpy as jnp
from jax import lax
from jax.sharding import PartitionSpec as P

HS = 128


def shifted(array, axis, by):
    devices = lax.axis_size(axis)
    pairs = [(i, i + by) for i in range(devices) if 0 <= i + by < devices]
    return lax.ppermute(array, axis, pairs)


def entering(value, axis, join, neutral):
    count, mine = (lax.axis_size(axis), lax.axis_index(axis))
    pieces = jax.tree.map(lambda part: lax.all_gather(part, axis), value)
    so_far = jax.tree.map(
        lambda part, zero: jnp.full_like(part, 0) + jnp.asarray(zero, part.dtype), value, neutral
    )

    def lap(position, so_far):
        longer = join(so_far, jax.tree.map(lambda part: part[position], pieces))
        return jax.tree.map(lambda new, old: jnp.where(position < mine, new, old), longer, so_far)

    return lax.fori_loop(0, count - 1, lap, so_far)


def pick_later(earlier, later):
    taken = later[0][0] > 0
    return (
        jnp.maximum(earlier[0], later[0]),
        jnp.where(taken, later[1], earlier[1]),
        jnp.where(taken, later[2], earlier[2]),
    )


def per_device(queries, keys, values, anchor_of, out_weight):
    frame = lax.axis_index("tm")
    dist = frame - anchor_of[frame]
    own_keys = keys[0]
    own_values = values[0]
    prev_keys, prev_values = shifted((own_keys, own_values), "tm", 1)
    flag = jnp.where(dist == 0, 1.0, 0.0).astype(jnp.bfloat16).reshape(1)
    empty = (jnp.zeros((1,), jnp.bfloat16), jnp.zeros_like(own_keys), jnp.zeros_like(own_values))
    marked, anchor_keys, anchor_values = entering(
        (flag, own_keys, own_values), "tm", pick_later, empty
    )
    tokens = own_keys.shape[0]
    heads_here = own_keys.shape[1] // HS
    key_rows = jnp.concatenate([own_keys, prev_keys, anchor_keys], 0).reshape(
        3 * tokens, heads_here, HS
    )
    value_rows = jnp.concatenate([own_values, prev_values, anchor_values], 0).reshape(
        3 * tokens, heads_here, HS
    )
    query_rows = queries[0].reshape(tokens, heads_here, HS)
    block = jnp.arange(3 * tokens, dtype=jnp.int32) // tokens
    present = (block == 0) | (block == 1) & (dist >= 1) | (block == 2) & (dist >= 2)
    outputs = []
    for which in range(heads_here):
        scores = jnp.dot(
            query_rows[:, which], key_rows[:, which].T, preferred_element_type=jnp.float32
        ) * HS ** (-0.5)
        scores = jnp.where(present[None, :], scores, -jnp.inf)
        top = jnp.max(scores, axis=-1, keepdims=True)
        expo = jnp.exp(scores - top)
        weights = (expo / jnp.sum(expo, axis=-1, keepdims=True)).astype(jnp.bfloat16)
        outputs.append(
            jnp.dot(weights, value_rows[:, which], preferred_element_type=jnp.float32).astype(
                jnp.bfloat16
            )
        )
    attended = jnp.concatenate(outputs, 1)
    share = lax.psum_scatter(
        jnp.dot(attended, out_weight, preferred_element_type=jnp.float32).astype(jnp.bfloat16),
        "head",
        scatter_dimension=0,
        tiled=True,
    )
    return share[None]


def solution(mesh):
    placed = (
        P("tm", None, "head"),
        P("tm", None, "head"),
        P("tm", None, "head"),
        P(),
        P("head", None),
    )
    return jax.shard_map(
        per_device, mesh=mesh, in_specs=placed, out_specs=P("tm", "head", None), check_vma=False
    )
```

profile of v0, /device:TPU:6, one launch (start us, length us, event | category | flops | bytes accessed | tf_op | source)
XLA Modules:
  0.0 835.6 jit_solution(14624638788721696858)
XLA Ops:
  9.1 1.9 collective-permute-start
  12.0 4.4 collective-permute-start.1
  21.5 246.4 %all-reduce = bf16[128]{0:T(256)(128)(2,1)S(1)} all-reduce(bf16[128]{0:T(256)(128)(2,1)S(1)} %dynamic-update-slice), channel_id=1, replica_groups=mesh['tm'=128,'head'=4] {'tm'}, use_global_device_ids=true, to_apply=%add | all-reduce | flops 128 | bytes 512
  268.0 215.0 %all-gather.5.cloned.1.call-done = bf16[128,128,512]{2,1,0:T(8,128)(2,1)} async-done(((bf16[1,128,512]{2,1,0:T(8,128)(2,1)}), bf16[128,128,512]{2,1,0:T(8,128)(2,1)}) %all-gather.5.cloned.1.call-update) | async-done | bytes 16777232 | tf_op jit(solution)/shard_map/all_gather | solution.py:17
  483.0 312.1 %while.16 = (s32[]{:T(128)}, bf16[128,512]{1,0:T(8,128)(2,1)S(1)}, bf16[128,512]{1,0:T(8,128)(2,1)S(1)}, s32[]{:T(128)}, bf16[128,1]{0,1:T(2,128)(2,1)S(1)}, /*i...) while((s32[]{:T(128)}, bf16[128,512]{1,0:T(8,128)(2,1)S(1)}, ...), condition=%wide.region_1.2_spmd.clone, body=%wide.region_0.1_spmd.clone.sunk | while | flops 393223 | bytes 786557 | solution.py:26
  483.7 1.8 select_select_fusion.3
  486.1 1.8 select_select_fusion.3
  488.6 1.8 select_select_fusion.3
  491.0 1.8 select_select_fusion.3
  493.5 1.8 select_select_fusion.3
  496.0 1.8 select_select_fusion.3
  498.4 1.8 select_select_fusion.3
  500.9 1.8 select_select_fusion.3
  503.3 1.8 select_select_fusion.3
  505.8 1.8 select_select_fusion.3
  508.2 1.8 select_select_fusion.3
  510.7 1.8 select_select_fusion.3
  513.2 1.8 select_select_fusion.3
  515.6 1.8 select_select_fusion.3
  518.1 1.8 select_select_fusion.3
  520.5 1.8 select_select_fusion.3
  523.0 1.8 select_select_fusion.3
  525.4 1.8 select_select_fusion.3
  527.9 1.8 select_select_fusion.3
  530.4 1.8 select_select_fusion.3
  532.8 1.8 select_select_fusion.3
  535.3 1.8 select_select_fusion.3
  537.7 1.8 select_select_fusion.3
  540.2 1.8 select_select_fusion.3
  542.6 1.8 select_select_fusion.3
  545.1 1.8 select_select_fusion.3
  547.6 1.8 select_select_fusion.3
  550.0 1.8 select_select_fusion.3
  552.5 1.8 select_select_fusion.3
  554.9 1.8 select_select_fusion.3
  557.4 1.8 select_select_fusion.3
  559.8 1.8 select_select_fusion.3
  562.3 1.8 select_select_fusion.3
  564.8 1.8 select_select_fusion.3
  567.2 1.8 select_select_fusion.3
  569.7 1.8 select_select_fusion.3
  572.1 1.8 select_select_fusion.3
  574.6 1.8 select_select_fusion.3
  577.0 1.8 select_select_fusion.3
  582.0 1.8 select_select_fusion.3
  594.3 1.8 select_select_fusion.3
  599.2 1.8 select_select_fusion.3
  611.5 1.8 select_select_fusion.3
  628.7 1.8 select_select_fusion.3
  640.9 1.8 select_select_fusion.3
  645.9 1.8 select_select_fusion.3
  658.1 1.8 select_select_fusion.3
  675.3 1.8 select_select_fusion.3
  687.6 1.8 select_select_fusion.3
  692.5 1.8 select_select_fusion.3
  704.8 1.8 select_select_fusion.3
  722.0 1.8 select_select_fusion.3
  734.3 1.8 select_select_fusion.3
  739.2 1.8 select_select_fusion.3
  751.5 1.8 select_select_fusion.3
  768.7 1.8 select_select_fusion.3
  781.0 1.8 select_select_fusion.3
  785.9 1.8 select_select_fusion.3
  799.5 29.5 %reduce-scatter.2.cloned.1.call-done = bf16[32,2048]{1,0:T(8,128)(2,1)} async-done(((bf16[128,2048]{1,0:T(8,128)(2,1)}), bf16[32,2048]{1,0:T(8,128)(2,1)}) %reduce-scatter.2.cloned.1.call-update) | async-done | bytes 131088 | tf_op jit(solution)/shard_map/reduce_scatter | solution.py:75
  (236 shorter events, 219.2 us)
Async XLA Ops:
  6.5 791.7 %copy-start = (bf16[512,2048]{1,0:T(8,128)(2,1)S(1)}, bf16[512,2048]{1,0:T(8,128)(2,1)}, u32[]{:S(2)}) copy-start(bf16[512,2048]{1,0:T(8,128)(2,1)} %param.11) | copy-start | bytes 6291460
  6.5 261.4 %all-gather.3.cloned.1.call-start = ((), (), s32[]{:S(2)}) async-start(), calls=%async_computation.1 | async-start | bytes 16908288 | tf_op jit(solution)/shard_map/all_gather | solution.py:17
  7.3 475.7 %all-gather.5.cloned.1.call-start = ((), (), s32[]{:S(2)}) async-start(), calls=%async_computation.2 | async-start | bytes 16908288 | tf_op jit(solution)/shard_map/all_gather | solution.py:17
  8.0 821.0 %reduce-scatter.2.cloned.1.call-start = ((), (), s32[]{:S(2)}) async-start(), calls=%async_computation.3 | async-start | bytes 655360 | tf_op jit(solution)/shard_map/reduce_scatter | solution.py:75
  9.1 786.1 %collective-permute-start = (bf16[128,512]{0,1:T(8,128)(2,1)S(1)}, bf16[128,512]{0,1:T(8,128)(2,1)S(1)}, u32[]{:S(2)}, u32[]{:S(2)}) collective-permute-start(bf16[128,512]{0,1:T(8,128)(2,1)S(1)} %bitcast.90), channel_id=1, source_target_pairs={{0,4},{4,8},{8,12},{12,16},{16,20},{20,24},{24,28},{28,32},{32,36}... | collective-permute-start | bytes 393224 | tf_op jit(solution)/shard_map/ppermute | solution.py:12
  12.0 785.1 %collective-permute-start.1 = (bf16[128,512]{0,1:T(8,128)(2,1)S(1)}, bf16[128,512]{0,1:T(8,128)(2,1)S(1)}, u32[]{:S(2)}, u32[]{:S(2)}) collective-permute-start(bf16[128,512]{0,1:T(8,128)(2,1)S(1)} %bitcast.88), channel_id=1, source_target_pairs={{0,4},{4,8},{8,12},{12,16},{16,20},{20,24},{24,28},{28,32},{32,36}... | collective-permute-start | bytes 393224 | tf_op jit(solution)/shard_map/ppermute | solution.py:12
  268.0 527.8 %copy-start.1 = (pred[384]{0:T(512)(128)(4,1)}, pred[384]{0:T(512)(128)(4,1)S(1)}, u32[]{:S(2)}) copy-start(pred[384]{0:T(512)(128)(4,1)S(1)} %fusion.22) | copy-start | bytes 1156
Sparse Core Ops, SparseCore 0:
  9.5 236.6 all-gather.2
  248.4 234.5 all-gather.4
  799.6 29.3 reduce-scatter.1
where the time goes:
time: 840 us; the launch traced here: 836 us
  other arithmetic  310 us (37%)
  waiting for transfers between devices  246 us (29%)
  blocking collectives  246 us (29%)
  between operations  13.9 us (2%)
    unnamed x1, blocking collectives  246 us
    select_n x127, other arithmetic, lap(): jnp.where(position < mine, new, old)  225 us
    all_gather x2, waiting for transfers between devices, entering(): pieces = jax.tree.map(lambda part: lax.all_gather(part, axis), value)  215 us
    gt x127, other arithmetic, pick_later(): taken = later[0][0] > 0  84.5 us
    reduce_scatter x1, waiting for transfers between devices, per_device(): lax.psum_scatter(jnp.dot(attended, out_weight, preferred_element_type=jnp...  29.5 us
  transfers between devices with their start and end apart: 5, of which 2 were waited for; matrix products, arithmetic and copies ran while one was open for 38% of the time, Pallas kernels for 0%

commit v1 on v0

v1 whole, which is shorter than its diff:
```python
import functools

import jax
import jax.numpy as jnp
from jax import lax
from jax.experimental import pallas as pl
from jax.experimental.pallas import tpu as pltpu
from jax.sharding import PartitionSpec as P

HS = 128
MESH = pl.DeviceIdType.MESH
F32 = jnp.float32
BF16 = jnp.bfloat16


def remote(src, dst, send_sem, recv_sem, device):
    return pltpu.make_async_remote_copy(
        src_ref=src,
        dst_ref=dst,
        send_sem=send_sem,
        recv_sem=recv_sem,
        device_id=device,
        device_id_type=MESH,
    )


def dot_nt(a, b):
    return lax.dot_general(a, b, (((1,), (1,)), ((), ())), preferred_element_type=F32)


def kernel(
    frames, groups,
    q_hbm, k_hbm, v_hbm, anchor_hbm, w_hbm, out_ref,
    anchor, q, own, prev, anc, pick, hand, w, att, acc, part, first, direct, chained, onward,
    load_sem, own_sem, w_sem,
    prev_send, prev_recv, pick_send, hand_send, anc_recv,
    first_send, first_recv, direct_send, direct_recv, chain_send, chain_recv,
):
    f = lax.axis_index("tm")
    h = lax.axis_index("head")
    tokens = q.shape[0]
    heads = q.shape[1] // HS
    chunks, _, width = part.shape
    rows = tokens // groups
    even = lax.rem(f, 2) == 0
    after, after2 = lax.rem(f + 1, frames), lax.rem(f + 2, frames)
    before, before2 = lax.rem(f + frames - 1, frames), lax.rem(f + frames - 2, frames)
    up, down = lax.rem(h + 1, groups), lax.rem(h + groups - 1, groups)
    far = lax.rem(h + 2, groups)

    barrier = pltpu.get_barrier_semaphore()
    for device in ((before, h), (f, up), (f, down)):
        pl.semaphore_signal(barrier, inc=1, device_id=device, device_id_type=MESH)

    @pl.when(even)
    def _():
        pl.semaphore_signal(barrier, inc=1, device_id=(before2, h), device_id_type=MESH)

    load_anchor = pltpu.make_async_copy(anchor_hbm, anchor, load_sem.at[0])
    load_q = pltpu.make_async_copy(q_hbm.at[0], q, load_sem.at[1])
    load_anchor.start()
    loads = []
    for c in range(heads):
        columns = pl.ds(c * HS, HS)
        loads.append([
            pltpu.make_async_copy(ref.at[0, :, columns], own.at[c, i], own_sem.at[c, i])
            for i, ref in enumerate((k_hbm, v_hbm))
        ])
        for copy in loads[-1]:
            copy.start()
    load_q.start()
    load_w = pltpu.make_async_copy(w_hbm, w, w_sem)
    load_w.start()

    pl.semaphore_wait(barrier, jnp.where(even, 4, 3))

    to_next = []
    for c in range(heads):
        columns = pl.ds(c * HS, HS)
        to_next.append([
            remote(ref.at[0, :, columns], prev.at[c, i], prev_send.at[c, i],
                   prev_recv.at[c, i], (after, h))
            for i, ref in enumerate((k_hbm, v_hbm))
        ])
        for copy in to_next[-1]:
            copy.start()

    load_anchor.wait()
    dist = f - anchor[f]
    next_dist = after - anchor[after]
    load_q.wait()
    scale = HS ** (-0.5)

    state = []
    picks = [remote(pick.at[c], anc.at[c], pick_send.at[c], anc_recv.at[c], (after2, h))
             for c in range(heads)]
    hands = [remote(hand.at[c], anc.at[c], hand_send.at[c], anc_recv.at[c], (after, h))
             for c in range(heads)]
    starts = jnp.full((tokens, HS), dist, jnp.int32) == 0
    for c in range(heads):
        for copy in loads[c]:
            copy.wait()
        for copy in to_next[c]:
            copy.wait_recv()

        @pl.when(even)
        def _():
            for i in range(2):
                pick[c, i] = jnp.where(starts, own[c, i], prev[c, i])
            picks[c].start()

    seen1 = jnp.full((tokens, tokens), dist, jnp.int32) >= 1
    seen2 = jnp.full((tokens, tokens), dist, jnp.int32) >= 2
    for c in range(heads):
        query = q[:, c * HS:(c + 1) * HS]
        s0 = dot_nt(query, own[c, 0]) * scale
        s1 = jnp.where(seen1, dot_nt(query, prev[c, 0]) * scale, -jnp.inf)
        top = jnp.max(jnp.maximum(s0, s1), axis=-1, keepdims=True)
        e0, e1 = jnp.exp(s0 - top), jnp.exp(s1 - top)
        total = jnp.sum(e0 + e1, axis=-1, keepdims=True)
        mixed = jnp.dot(e0.astype(BF16), own[c, 1], preferred_element_type=F32)
        mixed += jnp.dot(e1.astype(BF16), prev[c, 1], preferred_element_type=F32)
        state.append((top, total, mixed))

    takes_prev = jnp.full((tokens, HS), next_dist, jnp.int32) == 2
    for c in range(heads):
        picks[c].wait_recv()

        @pl.when(even)
        def _():
            for i in range(2):
                hand[c, i] = jnp.where(takes_prev, prev[c, i], anc[c, i])
            hands[c].start()

        query = q[:, c * HS:(c + 1) * HS]
        top, total, mixed = state[c]
        s2 = jnp.where(seen2, dot_nt(query, anc[c, 0]) * scale, -jnp.inf)
        peak = jnp.maximum(top, jnp.max(s2, axis=-1, keepdims=True))
        shrink = jnp.exp(top - peak)
        e2 = jnp.exp(s2 - peak)
        total = total * shrink + jnp.sum(e2, axis=-1, keepdims=True)
        mixed = mixed * shrink + jnp.dot(e2.astype(BF16), anc[c, 1], preferred_element_type=F32)
        att[:, c * HS:(c + 1) * HS] = (mixed / total).astype(BF16)
        if c == heads // 2:
            load_w.wait()
            half = (heads // 2) * HS
            for j in range(chunks):
                acc[j] = jnp.dot(att[:, :half], w[:half, j * width:(j + 1) * width],
                                 preferred_element_type=F32)

    def piece(group):
        return pl.ds(pl.multiple_of(group * rows, rows), rows)

    half = (heads // 2) * HS
    order = [j for pair in zip(range(chunks // 2), range(chunks // 2, chunks)) for j in pair]
    chain_to = [down if j < chunks // 2 else up for j in range(chunks)]
    direct_to = [up if j < chunks // 2 else down for j in range(chunks)]
    firsts = [remote(part.at[j, piece(far)], first.at[j], first_send.at[j], first_recv.at[j],
                     (f, chain_to[j])) for j in range(chunks)]
    directs = [remote(part.at[j, piece(direct_to[j])], direct.at[j], direct_send.at[j],
                      direct_recv.at[j], (f, direct_to[j])) for j in range(chunks)]
    chains = [remote(onward.at[j], chained.at[j], chain_send.at[j], chain_recv.at[j],
                     (f, chain_to[j])) for j in range(chunks)]
    for j in order:
        part[j] = (acc[j] + jnp.dot(att[:, half:], w[half:, j * width:(j + 1) * width],
                                    preferred_element_type=F32)).astype(BF16)
        firsts[j].start()
    for j in order:
        directs[j].start()
    for j in order:
        firsts[j].wait_recv()
        onward[j] = (part[j, piece(chain_to[j])].astype(F32) + first[j].astype(F32)).astype(BF16)
        chains[j].start()
    for j in order:
        directs[j].wait_recv()
        chains[j].wait_recv()
        out_ref[0, :, j * width:(j + 1) * width] = (
            part[j, piece(h)].astype(F32) + direct[j].astype(F32) + chained[j].astype(F32)
        ).astype(BF16)

    for c in range(heads):
        for copy in to_next[c]:
            copy.wait_send()
    for j in range(chunks):
        firsts[j].wait_send()
        directs[j].wait_send()
        chains[j].wait_send()

    @pl.when(even)
    def _():
        for c in range(heads):
            picks[c].wait_send()
            hands[c].wait_send()


def per_device(frames, groups, queries, keys, values, anchor_of, out_weight):
    _, tokens, wide = queries.shape
    heads = wide // HS
    depth, columns = out_weight.shape
    chunks = 4
    width = columns // chunks
    rows = tokens // groups
    block = pltpu.VMEM((heads, 2, tokens, HS), BF16)
    piece = pltpu.VMEM((chunks, rows, width), BF16)
    dma = pltpu.SemaphoreType.DMA
    hbm = pl.BlockSpec(memory_space=pl.ANY)
    return pl.pallas_call(
        functools.partial(kernel, frames, groups),
        out_shape=jax.ShapeDtypeStruct((1, rows, columns), BF16),
        in_specs=[hbm] * 5,
        out_specs=pl.BlockSpec(memory_space=pltpu.VMEM),
        scratch_shapes=[
            pltpu.SMEM(anchor_of.shape, jnp.int32),
            pltpu.VMEM((tokens, wide), BF16),
            block, block, block, block, block,
            pltpu.VMEM((depth, columns), BF16),
            pltpu.VMEM((tokens, wide), BF16),
            pltpu.VMEM((chunks, tokens, width), F32),
            pltpu.VMEM((chunks, tokens, width), BF16),
            piece, piece, piece, piece,
            dma((2,)), dma((heads, 2)), dma,
            dma((heads, 2)), dma((heads, 2)), dma((heads,)), dma((heads,)), dma((heads,)),
            dma((chunks,)), dma((chunks,)), dma((chunks,)), dma((chunks,)), dma((chunks,)),
            dma((chunks,)),
        ],
        compiler_params=pltpu.CompilerParams(collective_id=0, has_side_effects=True),
    )(queries, keys, values, anchor_of, out_weight)


def solution(mesh):
    placed = (
        P("tm", None, "head"),
        P("tm", None, "head"),
        P("tm", None, "head"),
        P(),
        P("head", None),
    )
    return jax.shard_map(
        functools.partial(per_device, mesh.shape["tm"], mesh.shape["head"]),
        mesh=mesh, in_specs=placed, out_specs=P("tm", "head", None), check_vma=False
    )
```

time: 840 us -> 39.6 us (0.05)
  the two profiles are of different devices: /device:TPU:6 before, /device:TPU:1 now
where the time goes in v1:
time: 39.6 us; the launch traced here: 39.5 us
  Pallas kernels  37.9 us (96%)
  local copies, waits for them, and re-layouts  1.57 us (4%)
    pallas_call x1, Pallas kernels, per_device(): pl.pallas_call(functools.partial(kernel, frames, groups), out_shape=jax.S...  37.9 us
    unnamed x1, local copies, waits for them, and re-layouts  1.57 us

profile of v1, /device:TPU:1, one launch (start us, length us, event | category | flops | bytes accessed | tf_op | source)
XLA Modules:
  0.0 39.5 jit_solution(12085493176973500181)
XLA Ops:
  0.0 37.9 %shard_map.55 = bf16[1,32,2048]{2,1,0:T(8,128)(2,1)} custom-call(bf16[1,128,512]{2,1,0:T(8,128)(2,1)} %q_hbm.1, bf16[1,128,512]{2,1,0:T(8,128)(2,1)} %k_hbm.1, bf16[1,128,512]{2,1,0:T(8,128)(2,1)} %v_hbm.1, s32[128]{0:T(128)} %anchor_hbm.1, bf16[512,2048]{1,0:T(8,128)(2,1)} %w_hbm.1), custom_call_target="tpu_custom_call" | custom-call | tf_op jit(solution)/shard_map/pallas_call | solution.py:207
  37.9 1.6 %copy.7 = bf16[1,32,2048]{2,1,0:T(8,128)(2,1)} copy(bf16[1,32,2048]{2,1,0:T(8,128)(2,1)} %shard_map.55) | data formatting | bytes 262144

commit v2 on v1

v2 whole, which is shorter than its diff:
```python
import functools

import jax
import jax.numpy as jnp
from jax import lax
from jax.experimental import pallas as pl
from jax.experimental.pallas import tpu as pltpu
from jax.sharding import PartitionSpec as P

HS = 128
MESH = pl.DeviceIdType.MESH
F32 = jnp.float32
BF16 = jnp.bfloat16


def remote(src, dst, send_sem, recv_sem, device):
    return pltpu.make_async_remote_copy(
        src_ref=src,
        dst_ref=dst,
        send_sem=send_sem,
        recv_sem=recv_sem,
        device_id=device,
        device_id_type=MESH,
    )


def dot_nt(a, b):
    return lax.dot_general(a, b, (((1,), (1,)), ((), ())), preferred_element_type=F32)


def plan_of(me, low, high):
    a, b = low
    c, d = high
    P = [("P", j, None) for j in range(4)]
    if me == 0:
        return [P[a], ("D", a, 1), P[b], ("D", b, 1), P[c], ("D", c, 1), ("D", c, 3),
                P[d], ("D", d, 1), ("D", d, 3), ("F", a, None), ("F", c, None),
                ("F", b, None), ("F", d, None), ("C", a, 3), ("C", b, 3)]
    if me == 1:
        return [P[c], ("D", c, 0), P[d], ("D", d, 0), P[a], ("F", a, None), ("D", a, 2),
                P[b], ("D", b, 2), ("F", c, None), ("C", a, 0), ("C", b, 0),
                ("F", b, None), ("F", d, None), ("C", c, 2), ("C", d, 2)]
    if me == 2:
        return [P[a], ("F", a, None), P[c], ("F", c, None), P[b], ("F", b, None),
                P[d], ("F", d, None), ("D", a, 3), ("D", b, 3),
                ("C", a, 1), ("C", b, 1), ("C", c, 1), ("C", d, 1), ("C", c, 3), ("C", d, 3)]
    return [P[a], ("D", a, 0), ("F", a, None), P[b], ("D", b, 0), ("F", b, None),
            P[c], ("F", c, None), P[d], ("F", d, None), ("D", c, 2), ("D", d, 2),
            ("C", c, 0), ("C", d, 0), ("C", a, 2), ("C", b, 2)]


def kernel(
    frames, groups,
    q_hbm, k_hbm, v_hbm, anchor_hbm, w_hbm, mine_ref, direct_ref, chained_ref,
    anchor, q, own, prev, anc, pick, hand, w, att, acc, part, first, onward,
    load_sem, own_sem, w_sem, mine_sem,
    prev_send, prev_recv, pick_send, hand_send, anc_recv,
    first_send, first_recv, direct_send, direct_recv, chain_send, chain_recv,
):
    f = lax.axis_index("tm")
    h = lax.axis_index("head")
    tokens = q.shape[0]
    heads = q.shape[1] // HS
    chunks, _, width = part.shape
    rows = tokens // groups
    even = lax.rem(f, 2) == 0
    has_next, has_second = f < frames - 1, even & (f < frames - 2)
    after, after2 = lax.rem(f + 1, frames), lax.rem(f + 2, frames)
    up, down = lax.rem(h + 1, groups), lax.rem(h + groups - 1, groups)

    barrier = pltpu.get_barrier_semaphore()

    @pl.when(f > 0)
    def _():
        pl.semaphore_signal(barrier, inc=1, device_id=(f - 1, h), device_id_type=MESH)

    @pl.when(even & (f > 1))
    def _():
        pl.semaphore_signal(barrier, inc=1, device_id=(f - 2, h), device_id_type=MESH)

    for device in ((f, up), (f, down)):
        pl.semaphore_signal(barrier, inc=1, device_id=device, device_id_type=MESH)

    load_anchor = pltpu.make_async_copy(anchor_hbm, anchor, load_sem.at[0])
    load_q = pltpu.make_async_copy(q_hbm.at[0], q, load_sem.at[1])
    load_w = pltpu.make_async_copy(w_hbm, w, w_sem)
    loads = [[
        pltpu.make_async_copy(ref.at[0, :, pl.ds(c * HS, HS)], own.at[c, i], own_sem.at[c, i])
        for i, ref in enumerate((k_hbm, v_hbm))
    ] for c in range(heads)]
    for c in range(heads):
        for copy in loads[c]:
            copy.start()
    load_anchor.start()
    load_q.start()
    load_w.start()

    @pl.when(f == 0)
    def _():
        prev[...] = jnp.zeros_like(prev)

    @pl.when(f < 2)
    def _():
        anc[...] = jnp.zeros_like(anc)

    for c in range(heads):
        for copy in loads[c]:
            copy.wait()
    pl.semaphore_wait(
        barrier, 2 + jnp.where(has_next, 1, 0) + jnp.where(has_second, 1, 0))

    to_next = [remote(own.at[c], prev.at[c], prev_send.at[c], prev_recv.at[c], (after, h))
               for c in range(heads)]
    picks = [remote(pick.at[c], anc.at[c], pick_send.at[c], anc_recv.at[c], (after2, h))
             for c in range(heads)]
    hands = [remote(hand.at[c], anc.at[c], hand_send.at[c], anc_recv.at[c], (after, h))
             for c in range(heads)]

    @pl.when(has_next)
    def _():
        for c in range(heads):
            to_next[c].start()

    load_anchor.wait()
    dist = f - anchor[f]
    next_dist = after - anchor[after]
    load_q.wait()
    scale = HS ** (-0.5)

    starts = jnp.full((tokens, HS), dist, jnp.int32) == 0
    for c in range(heads):
        @pl.when(f > 0)
        def _():
            to_next[c].wait_recv()

        @pl.when(has_second)
        def _():
            for i in range(2):
                pick[c, i] = jnp.where(starts, own[c, i], prev[c, i])
            picks[c].start()

    seen1 = jnp.full((tokens, tokens), dist, jnp.int32) >= 1
    seen2 = jnp.full((tokens, tokens), dist, jnp.int32) >= 2
    state = []
    for c in range(heads):
        query = q[:, c * HS:(c + 1) * HS]
        s0 = dot_nt(query, own[c, 0]) * scale
        s1 = jnp.where(seen1, dot_nt(query, prev[c, 0]) * scale, -jnp.inf)
        top = jnp.max(jnp.maximum(s0, s1), axis=-1, keepdims=True)
        e0, e1 = jnp.exp(s0 - top), jnp.exp(s1 - top)
        total = jnp.sum(e0 + e1, axis=-1, keepdims=True)
        mixed = jnp.dot(e0.astype(BF16), own[c, 1], preferred_element_type=F32)
        mixed += jnp.dot(e1.astype(BF16), prev[c, 1], preferred_element_type=F32)
        state.append((top, total, mixed))

    takes_prev = jnp.full((tokens, HS), next_dist, jnp.int32) == 2
    half = (heads // 2) * HS

    def arrive_even(c):
        @pl.when(even & (f > 1))
        def _():
            picks[c].wait_recv()
            for i in range(2):
                hand[c, i] = jnp.where(takes_prev, prev[c, i], anc[c, i])
            hands[c].start()

    def arrive_odd(c):
        @pl.when(jnp.logical_not(even) & (f > 1))
        def _():
            hands[c].wait_recv()

    for c in range(heads):
        arrive_even(c)
        if c == heads - 1:
            load_w.wait()
            for j in range(chunks):
                acc[j] = jnp.dot(att[:, :half], w[:half, j * width:(j + 1) * width],
                                 preferred_element_type=F32)
        arrive_odd(c)
        query = q[:, c * HS:(c + 1) * HS]
        top, total, mixed = state[c]
        s2 = jnp.where(seen2, dot_nt(query, anc[c, 0]) * scale, -jnp.inf)
        peak = jnp.maximum(top, jnp.max(s2, axis=-1, keepdims=True))
        shrink = jnp.exp(top - peak)
        e2 = jnp.exp(s2 - peak)
        total = total * shrink + jnp.sum(e2, axis=-1, keepdims=True)
        mixed = mixed * shrink + jnp.dot(e2.astype(BF16), anc[c, 1], preferred_element_type=F32)
        att[:, c * HS:(c + 1) * HS] = (mixed / total).astype(BF16)

    def columns(j):
        return pl.ds(j * width, width)

    def reduce(me):
        upper, lower, far = (me + 1) % groups, (me - 1) % groups, (me + 2) % groups

        def via(dest, j):
            return (dest + 1) % groups if j < chunks // 2 or dest == 1 else (dest - 1) % groups

        def piece(j, dest):
            return part.at[j, pl.ds(dest * rows, rows)]

        def slot(at, dest):
            return 0 if dest == (at - 1) % groups else 1

        def first_copy(j, source):
            dest = (source + 2) % groups
            at = via(dest, j)
            n = slot(at, dest)
            return remote(piece(j, dest), first.at[n, j], first_send.at[j], first_recv.at[n, j],
                          (f, at))

        def direct_copy(j, dest):
            return remote(piece(j, dest), direct_ref.at[0, :, columns(j)],
                          direct_send.at[0 if dest == lower else 1, j], direct_recv.at[j],
                          (f, dest))

        def chain_copy(j, dest):
            n = slot(me, dest)
            return remote(onward.at[n, j], chained_ref.at[0, :, columns(j)], chain_send.at[n, j],
                          chain_recv.at[j], (f, dest))

        def project(j):
            part[j] = (acc[j] + jnp.dot(att[:, half:], w[half:, j * width:(j + 1) * width],
                                        preferred_element_type=F32)).astype(BF16)

        def chain(j, dest):
            n = slot(me, dest)
            first_copy(j, (dest + 2) % groups).wait_recv()
            onward[n, j] = (part[j, dest * rows:(dest + 1) * rows].astype(F32)
                            + first[n, j].astype(F32)).astype(BF16)
            copy = chain_copy(j, dest)
            copy.start()
            sent.append(copy)

        def go(copy):
            copy.start()
            sent.append(copy)

        sent = []
        everyone = range(chunks)
        low, high = everyone[:chunks // 2], everyone[chunks // 2:]
        directs = [(j, d) for d in (lower, upper) for j in everyone if via(d, j) != me]
        chains = [(j, d) for d in (lower, upper) for j in everyone if via(d, j) == me]
        plan = plan_of(me, low, high)
        done = set()
        for step in plan:
            kind, j, d = step
            if kind == "P":
                project(j)
            elif kind == "F":
                go(first_copy(j, me))
            elif kind == "D":
                assert (j, d) in directs
                go(direct_copy(j, d))
            else:
                assert (j, d) in chains
                chain(j, d)
            assert step not in done
            done.add(step)
        assert len(done) == 2 * chunks + len(directs) + len(chains)

        keep = pltpu.make_async_copy
        copies = [keep(piece(j, me), mine_ref.at[0, :, columns(j)], mine_sem.at[j])
                  for j in everyone]
        for copy in copies:
            copy.start()
        for copy in copies:
            copy.wait()
        for j in everyone:
            direct_copy(j, lower).wait_recv()
            chain_copy(j, lower).wait_recv()
        for copy in sent:
            copy.wait_send()

    for me in range(groups):
        pl.when(h == me)(functools.partial(reduce, me))

    @pl.when(has_next)
    def _():
        for c in range(heads):
            to_next[c].wait_send()

    @pl.when(has_second)
    def _():
        for c in range(heads):
            picks[c].wait_send()

    @pl.when(even & (f > 1))
    def _():
        for c in range(heads):
            hands[c].wait_send()


def per_device(frames, groups, queries, keys, values, anchor_of, out_weight):
    _, tokens, wide = queries.shape
    heads = wide // HS
    depth, columns = out_weight.shape
    chunks = 4
    width = columns // chunks
    rows = tokens // groups
    block = pltpu.VMEM((heads, 2, tokens, HS), BF16)
    pieces = pltpu.VMEM((2, chunks, rows, width), BF16)
    dma = pltpu.SemaphoreType.DMA
    hbm = pl.BlockSpec(memory_space=pltpu.HBM)
    anywhere = pl.BlockSpec(memory_space=pl.ANY)
    share = jax.ShapeDtypeStruct((1, rows, columns), BF16)
    mine, direct, chained = pl.pallas_call(
        functools.partial(kernel, frames, groups),
        out_shape=[share] * 3,
        in_specs=[hbm] * 5,
        out_specs=[anywhere] * 3,
        scratch_shapes=[
            pltpu.SMEM(anchor_of.shape, jnp.int32),
            pltpu.VMEM((tokens, wide), BF16),
            block, block, block, block, block,
            pltpu.VMEM((depth, columns), BF16),
            pltpu.VMEM((tokens, wide), BF16),
            pltpu.VMEM((chunks, tokens, width), F32),
            pltpu.VMEM((chunks, tokens, width), BF16),
            pieces, pieces,
            dma((2,)), dma((heads, 2)), dma, dma((chunks,)),
            dma((heads,)), dma((heads,)), dma((heads,)), dma((heads,)), dma((heads,)),
            dma((chunks,)), dma((2, chunks)), dma((2, chunks)), dma((chunks,)),
            dma((2, chunks)), dma((chunks,)),
        ],
        compiler_params=pltpu.CompilerParams(
            collective_id=0, has_side_effects=True, vmem_limit_bytes=24 * 2**20),
    )(*(pltpu.with_memory_space_constraint(x, pltpu.HBM)
        for x in (queries, keys, values, anchor_of, out_weight)))
    return (mine.astype(F32) + direct.astype(F32) + chained.astype(F32)).astype(BF16)


def solution(mesh):
    placed = (
        P("tm", None, "head"),
        P("tm", None, "head"),
        P("tm", None, "head"),
        P(),
        P("head", None),
    )
    return jax.shard_map(
        functools.partial(per_device, mesh.shape["tm"], mesh.shape["head"]),
        mesh=mesh, in_specs=placed, out_specs=P("tm", "head", None), check_vma=False
    )
```

time: 39.6 us -> 35.3 us (0.89)
  the two profiles are of different devices: /device:TPU:1 before, /device:TPU:2 now
where the time goes in v2:
time: 35.3 us; the launch traced here: 35.2 us
  Pallas kernels  34.5 us (98%)
  other arithmetic  0.71 us (2%)
    pallas_call x1, Pallas kernels, per_device(): pl.pallas_call(functools.partial(kernel, frames, groups), out_shape=[shar...  34.5 us
    convert_element_type x1, other arithmetic, per_device(): (mine.astype(F32) + direct.astype(F32) + chained.astype(F32)).astype(BF16)  0.71 us

profile of v2, /device:TPU:2, one launch (start us, length us, event | category | flops | bytes accessed | tf_op | source)
XLA Modules:
  0.0 35.2 jit_solution(10571698729253660486)
XLA Ops:
  0.0 34.5 %shard_map.55 = (bf16[1,32,2048]{2,1,0:T(8,128)(2,1)S(1)}, bf16[1,32,2048]{2,1,0:T(8,128)(2,1)S(1)}, bf16[1,32,2048]{2,1,0:T(8,128)(2,1)S(1)}) custom-call(bf16[1,128,512]{2,1,0:T(8,128)(2,1)} %q_hbm.1, bf16[1,128,512]{2,1,0:T(8,128)(2,1)} %k_hbm.1, bf16[1,128,512]{2,1,0:T(8,128)(2,1)} %v_hbm.1, s32[128]{0:T(128)} %anchor_hbm.1, bf16[512,2048]{1,0:T(8,128)(2,1)} %w_hbm.1), custom_call_target="tpu_custom_call" | custom-call | tf_op jit(solution)/shard_map/pallas_call | solution.py:307
  34.5 0.7 %add_convert_fusion = bf16[1,32,2048]{2,1,0:T(8,128)(2,1)} fusion(bf16[1,32,2048]{2,1,0:T(8,128)(2,1)S(1)} %get-tuple-element.10, bf16[1,32,2048]{2,1,0:T(8,128)(2,1)S(1)} %get-tuple-element.9, bf16[1,32,2048]{2,1,0:T(8,128)(2,1)S(1)} %get-tuple-element.8), kind=kLoop, calls=%fused_computation | loop fusion | flops 393216 | bytes 524288 | tf_op jit(solution)/shard_map/convert_element_type | solution.py:330

commit v3 on v2

--- a/solution.py
+++ b/solution.py
@@ -29,32 +29,41 @@
 
 
 def plan_of(me, low, high):
-    a, b = low
-    c, d = high
-    P = [("P", j, None) for j in range(4)]
+    def project(js):
+        return [("P", j, None) for j in js]
+
+    def far(js):
+        return [("F", j, None) for j in js]
+
+    def near(js, dest):
+        return [("D", j, dest) for j in js]
+
+    def chain(js, dest):
+        return [("C", j, dest) for j in js]
+
+    def mix(*lists):
+        return [step for group in zip(*lists) for step in group]
+
+    cut = len(low) // 2
     if me == 0:
-        return [P[a], ("D", a, 1), P[b], ("D", b, 1), P[c], ("D", c, 1), ("D", c, 3),
-                P[d], ("D", d, 1), ("D", d, 3), ("F", a, None), ("F", c, None),
-                ("F", b, None), ("F", d, None), ("C", a, 3), ("C", b, 3)]
+        return (mix(project(low), near(low, 1)) + mix(project(high), near(high, 1), near(high, 3))
+                + mix(far(low), far(high)) + chain(low, 3))
     if me == 1:
-        return [P[c], ("D", c, 0), P[d], ("D", d, 0), P[a], ("F", a, None), ("D", a, 2),
-                P[b], ("D", b, 2), ("F", c, None), ("C", a, 0), ("C", b, 0),
-                ("F", b, None), ("F", d, None), ("C", c, 2), ("C", d, 2)]
+        return (mix(project(high), near(high, 0)) + mix(project(low), near(low, 2))
+                + far(low[:cut]) + far(high) + chain(low, 0) + far(low[cut:]) + chain(high, 2))
     if me == 2:
-        return [P[a], ("F", a, None), P[c], ("F", c, None), P[b], ("F", b, None),
-                P[d], ("F", d, None), ("D", a, 3), ("D", b, 3),
-                ("C", a, 1), ("C", b, 1), ("C", c, 1), ("C", d, 1), ("C", c, 3), ("C", d, 3)]
-    return [P[a], ("D", a, 0), ("F", a, None), P[b], ("D", b, 0), ("F", b, None),
-            P[c], ("F", c, None), P[d], ("F", d, None), ("D", c, 2), ("D", d, 2),
-            ("C", c, 0), ("C", d, 0), ("C", a, 2), ("C", b, 2)]
+        return (mix(project(low), far(low), project(high), far(high)) + near(low, 3)
+                + chain(low, 1) + chain(high, 1) + chain(high, 3))
+    return (mix(project(low), near(low, 0), far(low)) + mix(project(high), far(high))
+            + near(high, 2) + chain(high, 0) + chain(low, 2))
 
 
 def kernel(
     frames, groups,
     q_hbm, k_hbm, v_hbm, anchor_hbm, w_hbm, mine_ref, direct_ref, chained_ref,
-    anchor, q, own, prev, anc, pick, hand, w, att, acc, part, first, onward,
+    anchor, q, own, prev, prev2, start, pick, w, att, acc, part, first, onward,
     load_sem, own_sem, w_sem, mine_sem,
-    prev_send, prev_recv, pick_send, hand_send, anc_recv,
+    prev_send, prev_recv, prev2_send, prev2_recv, pick_send, start_send, start_recv, go_sem,
     first_send, first_recv, direct_send, direct_recv, chain_send, chain_recv,
 ):
     f = lax.axis_index("tm")
@@ -64,8 +73,9 @@
     chunks, _, width = part.shape
     rows = tokens // groups
     even = lax.rem(f, 2) == 0
-    has_next, has_second = f < frames - 1, even & (f < frames - 2)
-    after, after2 = lax.rem(f + 1, frames), lax.rem(f + 2, frames)
+    odd = jnp.logical_not(even)
+    has_next, picking = f < frames - 1, even & (f < frames - 3)
+    after, after3 = lax.rem(f + 1, frames), lax.rem(f + 3, frames)
     up, down = lax.rem(h + 1, groups), lax.rem(h + groups - 1, groups)
 
     barrier = pltpu.get_barrier_semaphore()
@@ -74,9 +84,13 @@
     def _():
         pl.semaphore_signal(barrier, inc=1, device_id=(f - 1, h), device_id_type=MESH)
 
+    @pl.when(odd & (f > 1))
+    def _():
+        pl.semaphore_signal(barrier, inc=1, device_id=(f - 3, h), device_id_type=MESH)
+
     @pl.when(even & (f > 1))
     def _():
-        pl.semaphore_signal(barrier, inc=1, device_id=(f - 2, h), device_id_type=MESH)
+        pl.semaphore_signal(barrier, inc=1, device_id=(f + 1, h), device_id_type=MESH)
 
     for device in ((f, up), (f, down)):
         pl.semaphore_signal(barrier, inc=1, device_id=device, device_id_type=MESH)
@@ -101,43 +115,49 @@
 
     @pl.when(f < 2)
     def _():
-        anc[...] = jnp.zeros_like(anc)
+        start[...] = jnp.zeros_like(start)
 
     for c in range(heads):
         for copy in loads[c]:
             copy.wait()
     pl.semaphore_wait(
-        barrier, 2 + jnp.where(has_next, 1, 0) + jnp.where(has_second, 1, 0))
-
-    to_next = [remote(own.at[c], prev.at[c], prev_send.at[c], prev_recv.at[c], (after, h))
-               for c in range(heads)]
-    picks = [remote(pick.at[c], anc.at[c], pick_send.at[c], anc_recv.at[c], (after2, h))
-             for c in range(heads)]
-    hands = [remote(hand.at[c], anc.at[c], hand_send.at[c], anc_recv.at[c], (after, h))
-             for c in range(heads)]
+        barrier, 2 + jnp.where(has_next, 1, 0) + jnp.where(picking, 1, 0)
+        + jnp.where(odd & (f > 1), 1, 0))
+
+    parts = [(c, i) for c in range(heads) for i in range(2)]
+    to_next = {p: remote(own.at[p], prev.at[p], prev_send.at[p], prev_recv.at[p], (after, h))
+               for p in parts}
+    passing = {p: remote(prev.at[p], prev2.at[p], prev2_send.at[p], prev2_recv.at[p], (after, h))
+               for p in parts}
+    picks = {p: remote(pick.at[p], start.at[p], pick_send.at[p], start_recv.at[p], (after3, h))
+             for p in parts}
+    backs = {p: remote(start.at[p], start.at[p], start_send.at[p], start_recv.at[p],
+                       (jnp.maximum(f - 1, 0), h)) for p in parts}
 
     @pl.when(has_next)
     def _():
-        for c in range(heads):
-            to_next[c].start()
+        for p in parts:
+            to_next[p].start()
 
     load_anchor.wait()
     dist = f - anchor[f]
-    next_dist = after - anchor[after]
     load_q.wait()
     scale = HS ** (-0.5)
 
     starts = jnp.full((tokens, HS), dist, jnp.int32) == 0
-    for c in range(heads):
+    for p in parts:
         @pl.when(f > 0)
         def _():
-            to_next[c].wait_recv()
-
-        @pl.when(has_second)
-        def _():
-            for i in range(2):
-                pick[c, i] = jnp.where(starts, own[c, i], prev[c, i])
-            picks[c].start()
+            to_next[p].wait_recv()
+
+        @pl.when(picking)
+        def _():
+            pick[p] = jnp.where(starts, own[p], prev[p])
+            picks[p].start()
+
+        @pl.when(even & (f > 1))
+        def _():
+            passing[p].start()
 
     seen1 = jnp.full((tokens, tokens), dist, jnp.int32) >= 1
     seen2 = jnp.full((tokens, tokens), dist, jnp.int32) >= 2
@@ -153,39 +173,58 @@
         mixed += jnp.dot(e1.astype(BF16), prev[c, 1], preferred_element_type=F32)
         state.append((top, total, mixed))
 
-    takes_prev = jnp.full((tokens, HS), next_dist, jnp.int32) == 2
+    takes_prev = jnp.full((tokens, HS), jnp.where(odd, dist, 0), jnp.int32) == 2
     half = (heads // 2) * HS
 
-    def arrive_even(c):
-        @pl.when(even & (f > 1))
-        def _():
-            picks[c].wait_recv()
-            for i in range(2):
-                hand[c, i] = jnp.where(takes_prev, prev[c, i], anc[c, i])
-            hands[c].start()
-
-    def arrive_odd(c):
-        @pl.when(jnp.logical_not(even) & (f > 1))
-        def _():
-            hands[c].wait_recv()
-
     for c in range(heads):
-        arrive_even(c)
         if c == heads - 1:
             load_w.wait()
             for j in range(chunks):
                 acc[j] = jnp.dot(att[:, :half], w[:half, j * width:(j + 1) * width],
                                  preferred_element_type=F32)
-        arrive_odd(c)
+
+        @pl.when(odd & (f > 1))
+        def _():
+            for i in range(2):
+                picks[c, i].wait_recv()
+                backs[c, i].start()
+            for i in range(2):
+                passing[c, i].wait_recv()
+
+        @pl.when(even & (f > 1))
+        def _():
+            for i in range(2):
+                backs[c, i].wait_recv()
+
         query = q[:, c * HS:(c + 1) * HS]
         top, total, mixed = state[c]
-        s2 = jnp.where(seen2, dot_nt(query, anc[c, 0]) * scale, -jnp.inf)
+        anchor_key = jnp.where(takes_prev, prev2[c, 0], start[c, 0])
+        anchor_value = jnp.where(takes_prev, prev2[c, 1], start[c, 1])
+        s2 = jnp.where(seen2, dot_nt(query, anchor_key) * scale, -jnp.inf)
         peak = jnp.maximum(top, jnp.max(s2, axis=-1, keepdims=True))
         shrink = jnp.exp(top - peak)
         e2 = jnp.exp(s2 - peak)
         total = total * shrink + jnp.sum(e2, axis=-1, keepdims=True)
-        mixed = mixed * shrink + jnp.dot(e2.astype(BF16), anc[c, 1], preferred_element_type=F32)
+        mixed = mixed * shrink + jnp.dot(e2.astype(BF16), anchor_value, preferred_element_type=F32)
         att[:, c * HS:(c + 1) * HS] = (mixed / total).astype(BF16)
+
+    @pl.when(has_next)
+    def _():
+        for p in parts:
+            to_next[p].wait_send()
+
+    @pl.when(picking)
+    def _():
+        for p in parts:
+            picks[p].wait_send()
+
+    @pl.when((f == 2) | (f == 3))
+    def _():
+        pl.semaphore_signal(go_sem, inc=1, device_id=(f - 2, h), device_id_type=MESH)
+
+    @pl.when(f < 2)
+    def _():
+        pl.semaphore_wait(go_sem, 1)
 
     def columns(j):
         return pl.ds(j * width, width)
@@ -275,27 +314,22 @@
     for me in range(groups):
         pl.when(h == me)(functools.partial(reduce, me))
 
-    @pl.when(has_next)
-    def _():
-        for c in range(heads):
-            to_next[c].wait_send()
-
-    @pl.when(has_second)
-    def _():
-        for c in range(heads):
-            picks[c].wait_send()
-
     @pl.when(even & (f > 1))
     def _():
-        for c in range(heads):
-            hands[c].wait_send()
+        for p in parts:
+            passing[p].wait_send()
+
+    @pl.when(odd & (f > 1))
+    def _():
+        for p in parts:
+            backs[p].wait_send()
 
 
 def per_device(frames, groups, queries, keys, values, anchor_of, out_weight):
     _, tokens, wide = queries.shape
     heads = wide // HS
     depth, columns = out_weight.shape
-    chunks = 4
+    chunks = 8
     width = columns // chunks
     rows = tokens // groups
     block = pltpu.VMEM((heads, 2, tokens, HS), BF16)
@@ -319,7 +353,7 @@
             pltpu.VMEM((chunks, tokens, width), BF16),
             pieces, pieces,
             dma((2,)), dma((heads, 2)), dma, dma((chunks,)),
-            dma((heads,)), dma((heads,)), dma((heads,)), dma((heads,)), dma((heads,)),
+            *[dma((heads, 2))] * 7, pltpu.SemaphoreType.REGULAR,
             dma((chunks,)), dma((2, chunks)), dma((2, chunks)), dma((chunks,)),
             dma((2, chunks)), dma((chunks,)),
         ],

time: 35.3 us -> 34.6 us (0.980)
  the two profiles are of different devices: /device:TPU:2 before, /device:TPU:96 now
where the time goes in v3:
time: 34.6 us; the launch traced here: 34.5 us
  Pallas kernels  33.8 us (98%)
  other arithmetic  0.71 us (2%)
    pallas_call x1, Pallas kernels, per_device(): pl.pallas_call(functools.partial(kernel, frames, groups), out_shape=[shar...  33.8 us
    convert_element_type x1, other arithmetic, per_device(): (mine.astype(F32) + direct.astype(F32) + chained.astype(F32)).astype(BF16)  0.71 us

profile of v3, /device:TPU:96, one launch (start us, length us, event | category | flops | bytes accessed | tf_op | source)
XLA Modules:
  0.0 34.5 jit_solution(11503663124596075233)
XLA Ops:
  0.0 33.8 %shard_map.55 = (bf16[1,32,2048]{2,1,0:T(8,128)(2,1)S(1)}, bf16[1,32,2048]{2,1,0:T(8,128)(2,1)S(1)}, bf16[1,32,2048]{2,1,0:T(8,128)(2,1)S(1)}) custom-call(bf16[1,128,512]{2,1,0:T(8,128)(2,1)} %q_hbm.1, bf16[1,128,512]{2,1,0:T(8,128)(2,1)} %k_hbm.1, bf16[1,128,512]{2,1,0:T(8,128)(2,1)} %v_hbm.1, s32[128]{0:T(128)} %anchor_hbm.1, bf16[512,2048]{1,0:T(8,128)(2,1)} %w_hbm.1), custom_call_target="tpu_custom_call" | custom-call | tf_op jit(solution)/shard_map/pallas_call | solution.py:341
  33.8 0.7 %add_convert_fusion = bf16[1,32,2048]{2,1,0:T(8,128)(2,1)} fusion(bf16[1,32,2048]{2,1,0:T(8,128)(2,1)S(1)} %get-tuple-element.10, bf16[1,32,2048]{2,1,0:T(8,128)(2,1)S(1)} %get-tuple-element.9, bf16[1,32,2048]{2,1,0:T(8,128)(2,1)S(1)} %get-tuple-element.8), kind=kLoop, calls=%fused_computation | loop fusion | flops 393216 | bytes 524288 | tf_op jit(solution)/shard_map/convert_element_type | solution.py:364

commit v4 on v3

--- a/solution.py
+++ b/solution.py
@@ -44,13 +44,12 @@
     def mix(*lists):
         return [step for group in zip(*lists) for step in group]
 
-    cut = len(low) // 2
     if me == 0:
-        return (mix(project(low), near(low, 1)) + mix(project(high), near(high, 1), near(high, 3))
-                + mix(far(low), far(high)) + chain(low, 3))
+        return (mix(project(high), far(high)) + mix(project(low), far(low))
+                + near(low, 1) + near(high, 1) + near(high, 3) + chain(low, 3))
     if me == 1:
-        return (mix(project(high), near(high, 0)) + mix(project(low), near(low, 2))
-                + far(low[:cut]) + far(high) + chain(low, 0) + far(low[cut:]) + chain(high, 2))
+        return (mix(project(low), far(low)) + mix(project(high), near(high, 0), far(high))
+                + near(low, 2) + chain(low, 0) + chain(high, 2))
     if me == 2:
         return (mix(project(low), far(low), project(high), far(high)) + near(low, 3)
                 + chain(low, 1) + chain(high, 1) + chain(high, 3))

time: 34.6 us -> 34.2 us (0.988)
  the two profiles are of different devices: /device:TPU:96 before, /device:TPU:224 now
where the time goes in v4:
time: 34.2 us; the launch traced here: 34.1 us
  Pallas kernels  33.4 us (98%)
  other arithmetic  0.71 us (2%)
    pallas_call x1, Pallas kernels, per_device(): pl.pallas_call(functools.partial(kernel, frames, groups), out_shape=[shar...  33.4 us
    convert_element_type x1, other arithmetic, per_device(): (mine.astype(F32) + direct.astype(F32) + chained.astype(F32)).astype(BF16)  0.71 us

profile of v4, /device:TPU:224, one launch (start us, length us, event | category | flops | bytes accessed | tf_op | source)
XLA Modules:
  0.0 34.1 jit_solution(13548656863525617138)
XLA Ops:
  0.0 33.4 %shard_map.55 = (bf16[1,32,2048]{2,1,0:T(8,128)(2,1)S(1)}, bf16[1,32,2048]{2,1,0:T(8,128)(2,1)S(1)}, bf16[1,32,2048]{2,1,0:T(8,128)(2,1)S(1)}) custom-call(bf16[1,128,512]{2,1,0:T(8,128)(2,1)} %q_hbm.1, bf16[1,128,512]{2,1,0:T(8,128)(2,1)} %k_hbm.1, bf16[1,128,512]{2,1,0:T(8,128)(2,1)} %v_hbm.1, s32[128]{0:T(128)} %anchor_hbm.1, bf16[512,2048]{1,0:T(8,128)(2,1)} %w_hbm.1), custom_call_target="tpu_custom_call" | custom-call | tf_op jit(solution)/shard_map/pallas_call | solution.py:340
  33.4 0.7 %add_convert_fusion = bf16[1,32,2048]{2,1,0:T(8,128)(2,1)} fusion(bf16[1,32,2048]{2,1,0:T(8,128)(2,1)S(1)} %get-tuple-element.10, bf16[1,32,2048]{2,1,0:T(8,128)(2,1)S(1)} %get-tuple-element.9, bf16[1,32,2048]{2,1,0:T(8,128)(2,1)S(1)} %get-tuple-element.8), kind=kLoop, calls=%fused_computation | loop fusion | flops 393216 | bytes 524288 | tf_op jit(solution)/shard_map/convert_element_type | solution.py:363

commit v5 on v4

--- a/solution.py
+++ b/solution.py
@@ -46,13 +46,14 @@
 
     if me == 0:
         return (mix(project(high), far(high)) + mix(project(low), far(low))
-                + near(low, 1) + near(high, 1) + near(high, 3) + chain(low, 3))
+                + near(low, 1) + near(high[:-1], 1) + near(high, 3) + chain(high[-1:], 1)
+                + chain(low, 3))
     if me == 1:
         return (mix(project(low), far(low)) + mix(project(high), near(high, 0), far(high))
                 + near(low, 2) + chain(low, 0) + chain(high, 2))
     if me == 2:
         return (mix(project(low), far(low), project(high), far(high)) + near(low, 3)
-                + chain(low, 1) + chain(high, 1) + chain(high, 3))
+                + near(high[-1:], 1) + chain(low, 1) + chain(high[:-1], 1) + chain(high, 3))
     return (mix(project(low), near(low, 0), far(low)) + mix(project(high), far(high))
             + near(high, 2) + chain(high, 0) + chain(low, 2))
 
@@ -232,7 +233,8 @@
         upper, lower, far = (me + 1) % groups, (me - 1) % groups, (me + 2) % groups
 
         def via(dest, j):
-            return (dest + 1) % groups if j < chunks // 2 or dest == 1 else (dest - 1) % groups
+            onward_up = j >= (chunks - 1 if dest == 1 else chunks // 2)
+            return (dest - 1 if onward_up else dest + 1) % groups
 
         def piece(j, dest):
             return part.at[j, pl.ds(dest * rows, rows)]

time: 34.2 us -> 33.5 us (0.980)
  the two profiles are of different devices: /device:TPU:224 before, /device:TPU:40 now
where the time goes in v5:
time: 33.5 us; the launch traced here: 33.4 us
  Pallas kernels  32.6 us (97%)
  other arithmetic  0.71 us (2%)
    pallas_call x1, Pallas kernels, per_device(): pl.pallas_call(functools.partial(kernel, frames, groups), out_shape=[shar...  32.6 us
    convert_element_type x1, other arithmetic, per_device(): (mine.astype(F32) + direct.astype(F32) + chained.astype(F32)).astype(BF16)  0.71 us

profile of v5, /device:TPU:40, one launch (start us, length us, event | category | flops | bytes accessed | tf_op | source)
XLA Modules:
  0.0 33.4 jit_solution(14699996969278521350)
XLA Ops:
  0.0 32.6 %shard_map.55 = (bf16[1,32,2048]{2,1,0:T(8,128)(2,1)S(1)}, bf16[1,32,2048]{2,1,0:T(8,128)(2,1)S(1)}, bf16[1,32,2048]{2,1,0:T(8,128)(2,1)S(1)}) custom-call(bf16[1,128,512]{2,1,0:T(8,128)(2,1)} %q_hbm.1, bf16[1,128,512]{2,1,0:T(8,128)(2,1)} %k_hbm.1, bf16[1,128,512]{2,1,0:T(8,128)(2,1)} %v_hbm.1, s32[128]{0:T(128)} %anchor_hbm.1, bf16[512,2048]{1,0:T(8,128)(2,1)} %w_hbm.1), custom_call_target="tpu_custom_call" | custom-call | tf_op jit(solution)/shard_map/pallas_call | solution.py:342
  32.6 0.7 %add_convert_fusion = bf16[1,32,2048]{2,1,0:T(8,128)(2,1)} fusion(bf16[1,32,2048]{2,1,0:T(8,128)(2,1)S(1)} %get-tuple-element.10, bf16[1,32,2048]{2,1,0:T(8,128)(2,1)S(1)} %get-tuple-element.9, bf16[1,32,2048]{2,1,0:T(8,128)(2,1)S(1)} %get-tuple-element.8), kind=kLoop, calls=%fused_computation | loop fusion | flops 393216 | bytes 524288 | tf_op jit(solution)/shard_map/convert_element_type | solution.py:365

commit v6 on v5

--- a/solution.py
+++ b/solution.py
@@ -70,7 +70,7 @@
     h = lax.axis_index("head")
     tokens = q.shape[0]
     heads = q.shape[1] // HS
-    chunks, _, width = part.shape
+    chunks, _, width = acc.shape
     rows = tokens // groups
     even = lax.rem(f, 2) == 0
     odd = jnp.logical_not(even)
@@ -125,19 +125,19 @@
         + jnp.where(odd & (f > 1), 1, 0))
 
     parts = [(c, i) for c in range(heads) for i in range(2)]
-    to_next = {p: remote(own.at[p], prev.at[p], prev_send.at[p], prev_recv.at[p], (after, h))
-               for p in parts}
-    passing = {p: remote(prev.at[p], prev2.at[p], prev2_send.at[p], prev2_recv.at[p], (after, h))
-               for p in parts}
-    picks = {p: remote(pick.at[p], start.at[p], pick_send.at[p], start_recv.at[p], (after3, h))
-             for p in parts}
-    backs = {p: remote(start.at[p], start.at[p], start_send.at[p], start_recv.at[p],
-                       (jnp.maximum(f - 1, 0), h)) for p in parts}
+    to_next = [remote(own.at[c], prev.at[c], prev_send.at[c], prev_recv.at[c], (after, h))
+               for c in range(heads)]
+    passing = [remote(prev.at[c], prev2.at[c], prev2_send.at[c], prev2_recv.at[c], (after, h))
+               for c in range(heads)]
+    picks = [remote(pick.at[c], start.at[c], pick_send.at[c], start_recv.at[c], (after3, h))
+             for c in range(heads)]
+    backs = [remote(start.at[c], start.at[c], start_send.at[c], start_recv.at[c],
+                    (jnp.maximum(f - 1, 0), h)) for c in range(heads)]
 
     @pl.when(has_next)
     def _():
-        for p in parts:
-            to_next[p].start()
+        for copy in to_next:
+            copy.start()
 
     load_anchor.wait()
     dist = f - anchor[f]
@@ -146,18 +146,21 @@
 
     starts = jnp.full((tokens, HS), dist, jnp.int32) == 0
     for p in parts:
-        @pl.when(f > 0)
-        def _():
-            to_next[p].wait_recv()
+        if p[1] == 0:
+            @pl.when(f > 0)
+            def _():
+                to_next[p[0]].wait_recv()
 
         @pl.when(picking)
         def _():
             pick[p] = jnp.where(starts, own[p], prev[p])
-            picks[p].start()
-
-        @pl.when(even & (f > 1))
-        def _():
-            passing[p].start()
+            if p[1] == 1:
+                picks[p[0]].start()
+
+        if p[1] == 1:
+            @pl.when(even & (f > 1))
+            def _():
+                passing[p[0]].start()
 
     seen1 = jnp.full((tokens, tokens), dist, jnp.int32) >= 1
     seen2 = jnp.full((tokens, tokens), dist, jnp.int32) >= 2
@@ -185,16 +188,13 @@
 
         @pl.when(odd & (f > 1))
         def _():
-            for i in range(2):
-                picks[c, i].wait_recv()
-                backs[c, i].start()
-            for i in range(2):
-                passing[c, i].wait_recv()
+            picks[c].wait_recv()
+            backs[c].start()
+            passing[c].wait_recv()
 
         @pl.when(even & (f > 1))
         def _():
-            for i in range(2):
-                backs[c, i].wait_recv()
+            backs[c].wait_recv()
 
         query = q[:, c * HS:(c + 1) * HS]
         top, total, mixed = state[c]
@@ -210,13 +210,13 @@
 
     @pl.when(has_next)
     def _():
-        for p in parts:
-            to_next[p].wait_send()
+        for copy in to_next:
+            copy.wait_send()
 
     @pl.when(picking)
     def _():
-        for p in parts:
-            picks[p].wait_send()
+        for copy in picks:
+            copy.wait_send()
 
     @pl.when((f == 2) | (f == 3))
     def _():
@@ -237,7 +237,7 @@
             return (dest - 1 if onward_up else dest + 1) % groups
 
         def piece(j, dest):
-            return part.at[j, pl.ds(dest * rows, rows)]
+            return part.at[pl.ds(dest * rows, rows), columns(j)]
 
         def slot(at, dest):
             return 0 if dest == (at - 1) % groups else 1
@@ -246,28 +246,41 @@
             dest = (source + 2) % groups
             at = via(dest, j)
             n = slot(at, dest)
-            return remote(piece(j, dest), first.at[n, j], first_send.at[j], first_recv.at[n, j],
+            return remote(piece(j, dest), first.at[n, :, columns(j)], first_send.at[j], first_recv.at[n, j],
                           (f, at))
 
-        def direct_copy(j, dest):
-            return remote(piece(j, dest), direct_ref.at[0, :, columns(j)],
-                          direct_send.at[0 if dest == lower else 1, j], direct_recv.at[j],
-                          (f, dest))
+        def direct_copy(run, dest):
+            at = pl.ds(run[0] * width, len(run) * width)
+            return remote(part.at[pl.ds(dest * rows, rows), at], direct_ref.at[0, :, at],
+                          direct_send.at[0 if dest == lower else 1, run[0]],
+                          direct_recv.at[run[0]], (f, dest))
+
+        def runs_to(dest):
+            source = [(dest - 1) % groups if via(dest, j) != (dest - 1) % groups
+                      else (dest + 1) % groups for j in everyone]
+            runs = []
+            for j in everyone:
+                if runs and len(runs[-1]) < 4 and source[runs[-1][0]] == source[j]:
+                    runs[-1].append(j)
+                else:
+                    runs.append([j])
+            return runs
 
         def chain_copy(j, dest):
             n = slot(me, dest)
-            return remote(onward.at[n, j], chained_ref.at[0, :, columns(j)], chain_send.at[n, j],
+            return remote(onward.at[n, :, columns(j)], chained_ref.at[0, :, columns(j)], chain_send.at[n, j],
                           chain_recv.at[j], (f, dest))
 
         def project(j):
-            part[j] = (acc[j] + jnp.dot(att[:, half:], w[half:, j * width:(j + 1) * width],
+            part[:, j * width:(j + 1) * width] = (acc[j] + jnp.dot(att[:, half:], w[half:, j * width:(j + 1) * width],
                                         preferred_element_type=F32)).astype(BF16)
 
         def chain(j, dest):
             n = slot(me, dest)
             first_copy(j, (dest + 2) % groups).wait_recv()
-            onward[n, j] = (part[j, dest * rows:(dest + 1) * rows].astype(F32)
-                            + first[n, j].astype(F32)).astype(BF16)
+            at = slice(j * width, (j + 1) * width)
+            onward[n, :, at] = (part[dest * rows:(dest + 1) * rows, at].astype(F32)
+                                + first[n, :, at].astype(F32)).astype(BF16)
             copy = chain_copy(j, dest)
             copy.start()
             sent.append(copy)
@@ -276,7 +289,7 @@
             copy.start()
             sent.append(copy)
 
-        sent = []
+        sent, waiting = [], []
         everyone = range(chunks)
         low, high = everyone[:chunks // 2], everyone[chunks // 2:]
         directs = [(j, d) for d in (lower, upper) for j in everyone if via(d, j) != me]
@@ -291,7 +304,10 @@
                 go(first_copy(j, me))
             elif kind == "D":
                 assert (j, d) in directs
-                go(direct_copy(j, d))
+                waiting.append((j, d))
+                run = next(r for r in runs_to(d) if j in r)
+                if all((k, d) in waiting for k in run):
+                    go(direct_copy(run, d))
             else:
                 assert (j, d) in chains
                 chain(j, d)
@@ -300,14 +316,14 @@
         assert len(done) == 2 * chunks + len(directs) + len(chains)
 
         keep = pltpu.make_async_copy
-        copies = [keep(piece(j, me), mine_ref.at[0, :, columns(j)], mine_sem.at[j])
-                  for j in everyone]
-        for copy in copies:
-            copy.start()
-        for copy in copies:
-            copy.wait()
+        copy = keep(part.at[pl.ds(me * rows, rows)], mine_ref.at[0], mine_sem)
+        copy.start()
+        copy.wait()
+        for run in runs_to(me):
+            at = pl.ds(run[0] * width, len(run) * width)
+            remote(part.at[pl.ds(me * rows, rows), at], direct_ref.at[0, :, at],
+                   direct_send.at[0, run[0]], direct_recv.at[run[0]], (f, lower)).wait_recv()
         for j in everyone:
-            direct_copy(j, lower).wait_recv()
             chain_copy(j, lower).wait_recv()
         for copy in sent:
             copy.wait_send()
@@ -317,13 +333,13 @@
 
     @pl.when(even & (f > 1))
     def _():
-        for p in parts:
-            passing[p].wait_send()
+        for copy in passing:
+            copy.wait_send()
 
     @pl.when(odd & (f > 1))
     def _():
-        for p in parts:
-            backs[p].wait_send()
+        for copy in backs:
+            copy.wait_send()
 
 
 def per_device(frames, groups, queries, keys, values, anchor_of, out_weight):
@@ -334,7 +350,7 @@
     width = columns // chunks
     rows = tokens // groups
     block = pltpu.VMEM((heads, 2, tokens, HS), BF16)
-    pieces = pltpu.VMEM((2, chunks, rows, width), BF16)
+    pieces = pltpu.VMEM((2, rows, columns), BF16)
     dma = pltpu.SemaphoreType.DMA
     hbm = pl.BlockSpec(memory_space=pltpu.HBM)
     anywhere = pl.BlockSpec(memory_space=pl.ANY)
@@ -351,10 +367,10 @@
             pltpu.VMEM((depth, columns), BF16),
             pltpu.VMEM((tokens, wide), BF16),
             pltpu.VMEM((chunks, tokens, width), F32),
-            pltpu.VMEM((chunks, tokens, width), BF16),
+            pltpu.VMEM((tokens, columns), BF16),
             pieces, pieces,
-            dma((2,)), dma((heads, 2)), dma, dma((chunks,)),
-            *[dma((heads, 2))] * 7, pltpu.SemaphoreType.REGULAR,
+            dma((2,)), dma((heads, 2)), dma, dma,
+            *[dma((heads,))] * 7, pltpu.SemaphoreType.REGULAR,
             dma((chunks,)), dma((2, chunks)), dma((2, chunks)), dma((chunks,)),
             dma((2, chunks)), dma((chunks,)),
         ],

time: 33.5 us -> 33.2 us (level)
  the two profiles are of different devices: /device:TPU:40 before, /device:TPU:96 now
where the time goes in v6:
time: 33.2 us; the launch traced here: 33.1 us
  Pallas kernels  32.4 us (98%)
  other arithmetic  0.71 us (2%)
    pallas_call x1, Pallas kernels, per_device(): pl.pallas_call(functools.partial(kernel, frames, groups), out_shape=[shar...  32.4 us
    convert_element_type x1, other arithmetic, per_device(): (mine.astype(F32) + direct.astype(F32) + chained.astype(F32)).astype(BF16)  0.71 us

profile of v6, /device:TPU:96, one launch (start us, length us, event | category | flops | bytes accessed | tf_op | source)
XLA Modules:
  0.0 33.1 jit_solution(8799184465520191737)
XLA Ops:
  0.0 32.4 %shard_map.55 = (bf16[1,32,2048]{2,1,0:T(8,128)(2,1)S(1)}, bf16[1,32,2048]{2,1,0:T(8,128)(2,1)S(1)}, bf16[1,32,2048]{2,1,0:T(8,128)(2,1)S(1)}) custom-call(bf16[1,128,512]{2,1,0:T(8,128)(2,1)} %q_hbm.1, bf16[1,128,512]{2,1,0:T(8,128)(2,1)} %k_hbm.1, bf16[1,128,512]{2,1,0:T(8,128)(2,1)} %v_hbm.1, s32[128]{0:T(128)} %anchor_hbm.1, bf16[512,2048]{1,0:T(8,128)(2,1)} %w_hbm.1), custom_call_target="tpu_custom_call" | custom-call | tf_op jit(solution)/shard_map/pallas_call | solution.py:358
  32.4 0.7 %add_convert_fusion = bf16[1,32,2048]{2,1,0:T(8,128)(2,1)} fusion(bf16[1,32,2048]{2,1,0:T(8,128)(2,1)S(1)} %get-tuple-element.10, bf16[1,32,2048]{2,1,0:T(8,128)(2,1)S(1)} %get-tuple-element.9, bf16[1,32,2048]{2,1,0:T(8,128)(2,1)S(1)} %get-tuple-element.8), kind=kLoop, calls=%fused_computation | loop fusion | flops 393216 | bytes 524288 | tf_op jit(solution)/shard_map/convert_element_type | solution.py:381

commit v7 on v6

--- a/solution.py
+++ b/solution.py
@@ -236,21 +236,24 @@
             onward_up = j >= (chunks - 1 if dest == 1 else chunks // 2)
             return (dest - 1 if onward_up else dest + 1) % groups
 
-        def piece(j, dest):
-            return part.at[pl.ds(dest * rows, rows), columns(j)]
+        def run_of(j, dest):
+            length = 4 if dest > 1 else 1
+            return range(j // length * length, (j // length + 1) * length)
+
+        def span(run):
+            return pl.ds(run[0] * width, len(run) * width)
 
         def slot(at, dest):
             return 0 if dest == (at - 1) % groups else 1
 
-        def first_copy(j, source):
-            dest = (source + 2) % groups
-            at = via(dest, j)
+        def first_copy(run, dest):
+            at = via(dest, run[0])
             n = slot(at, dest)
-            return remote(piece(j, dest), first.at[n, :, columns(j)], first_send.at[j], first_recv.at[n, j],
-                          (f, at))
+            return remote(part.at[pl.ds(dest * rows, rows), span(run)], first.at[n, :, span(run)],
+                          first_send.at[run[0]], first_recv.at[n, run[0]], (f, at))
 
         def direct_copy(run, dest):
-            at = pl.ds(run[0] * width, len(run) * width)
+            at = span(run)
             return remote(part.at[pl.ds(dest * rows, rows), at], direct_ref.at[0, :, at],
                           direct_send.at[0 if dest == lower else 1, run[0]],
                           direct_recv.at[run[0]], (f, dest))
@@ -266,24 +269,22 @@
                     runs.append([j])
             return runs
 
-        def chain_copy(j, dest):
-            n = slot(me, dest)
-            return remote(onward.at[n, :, columns(j)], chained_ref.at[0, :, columns(j)], chain_send.at[n, j],
-                          chain_recv.at[j], (f, dest))
+        def chain_copy(run, source, dest):
+            n = slot(source, dest)
+            return remote(onward.at[n, :, span(run)], chained_ref.at[0, :, span(run)],
+                          chain_send.at[n, run[0]], chain_recv.at[run[0]], (f, dest))
 
         def project(j):
             part[:, j * width:(j + 1) * width] = (acc[j] + jnp.dot(att[:, half:], w[half:, j * width:(j + 1) * width],
                                         preferred_element_type=F32)).astype(BF16)
 
-        def chain(j, dest):
+        def chain(run, dest):
             n = slot(me, dest)
-            first_copy(j, (dest + 2) % groups).wait_recv()
-            at = slice(j * width, (j + 1) * width)
+            first_copy(run, dest).wait_recv()
+            at = slice(run[0] * width, (run[-1] + 1) * width)
             onward[n, :, at] = (part[dest * rows:(dest + 1) * rows, at].astype(F32)
                                 + first[n, :, at].astype(F32)).astype(BF16)
-            copy = chain_copy(j, dest)
-            copy.start()
-            sent.append(copy)
+            go(chain_copy(run, me, dest))
 
         def go(copy):
             copy.start()
@@ -301,7 +302,8 @@
             if kind == "P":
                 project(j)
             elif kind == "F":
-                go(first_copy(j, me))
+                if j == run_of(j, far)[-1]:
+                    go(first_copy(run_of(j, far), far))
             elif kind == "D":
                 assert (j, d) in directs
                 waiting.append((j, d))
@@ -310,7 +312,8 @@
                     go(direct_copy(run, d))
             else:
                 assert (j, d) in chains
-                chain(j, d)
+                if j == run_of(j, d)[-1]:
+                    chain(run_of(j, d), d)
             assert step not in done
             done.add(step)
         assert len(done) == 2 * chunks + len(directs) + len(chains)
@@ -320,11 +323,13 @@
         copy.start()
         copy.wait()
         for run in runs_to(me):
-            at = pl.ds(run[0] * width, len(run) * width)
+            at = span(run)
             remote(part.at[pl.ds(me * rows, rows), at], direct_ref.at[0, :, at],
                    direct_send.at[0, run[0]], direct_recv.at[run[0]], (f, lower)).wait_recv()
         for j in everyone:
-            chain_copy(j, lower).wait_recv()
+            if j == run_of(j, me)[0]:
+                remote(onward.at[0, :, span(run_of(j, me))], chained_ref.at[0, :, span(run_of(j, me))],
+                       chain_send.at[0, j], chain_recv.at[j], (f, lower)).wait_recv()
         for copy in sent:
             copy.wait_send()
 

time: 33.2 us -> 32.8 us (0.988)
  the two profiles are of different devices: /device:TPU:96 before, /device:TPU:224 now
where the time goes in v7:
time: 32.8 us; the launch traced here: 32.7 us
  Pallas kernels  32 us (98%)
  other arithmetic  0.71 us (2%)
    pallas_call x1, Pallas kernels, per_device(): pl.pallas_call(functools.partial(kernel, frames, groups), out_shape=[shar...  32 us
    convert_element_type x1, other arithmetic, per_device(): (mine.astype(F32) + direct.astype(F32) + chained.astype(F32)).astype(BF16)  0.71 us

profile of v7, /device:TPU:224, one launch (start us, length us, event | category | flops | bytes accessed | tf_op | source)
XLA Modules:
  0.0 32.7 jit_solution(16108748054878250212)
XLA Ops:
  0.0 32.0 %shard_map.55 = (bf16[1,32,2048]{2,1,0:T(8,128)(2,1)S(1)}, bf16[1,32,2048]{2,1,0:T(8,128)(2,1)S(1)}, bf16[1,32,2048]{2,1,0:T(8,128)(2,1)S(1)}) custom-call(bf16[1,128,512]{2,1,0:T(8,128)(2,1)} %q_hbm.1, bf16[1,128,512]{2,1,0:T(8,128)(2,1)} %k_hbm.1, bf16[1,128,512]{2,1,0:T(8,128)(2,1)} %v_hbm.1, s32[128]{0:T(128)} %anchor_hbm.1, bf16[512,2048]{1,0:T(8,128)(2,1)} %w_hbm.1), custom_call_target="tpu_custom_call" | custom-call | tf_op jit(solution)/shard_map/pallas_call | solution.py:363
  32.0 0.7 %add_convert_fusion = bf16[1,32,2048]{2,1,0:T(8,128)(2,1)} fusion(bf16[1,32,2048]{2,1,0:T(8,128)(2,1)S(1)} %get-tuple-element.10, bf16[1,32,2048]{2,1,0:T(8,128)(2,1)S(1)} %get-tuple-element.9, bf16[1,32,2048]{2,1,0:T(8,128)(2,1)S(1)} %get-tuple-element.8), kind=kLoop, calls=%fused_computation | loop fusion | flops 393216 | bytes 524288 | tf_op jit(solution)/shard_map/convert_element_type | solution.py:386
